TPU v7x, 512 devices: a whole 4x8x8 slice. The times are simulated.
512 devices in a mesh: seq: 64 (over y_hi, z, core), tp: 8 (over x, y_lo).
Axes of the slice: x: 4, y: 8 (y_hi: 4, y_lo: 2; y = y_hi * 2 + y_lo), z: 8, core: 2. Of those that a mesh axis runs over, the one named last changes fastest.
Arguments:
- resid: bfloat16 [8192, 2048], P('seq'), may hold values from -1.5 to 1.5
- query: bfloat16 [8192, 1024], P('seq', 'tp'), may hold values from -6 to 6
- key_new: bfloat16 [8192, 1024], P('seq', 'tp'), may hold values from -6 to 6
- value_new: bfloat16 [8192, 1024], P('seq', 'tp'), may hold values from -6 to 6
- key_cache: bfloat16 [1024, 1024], P('seq', 'tp'), may hold values from -6 to 6
- value_cache: bfloat16 [1024, 1024], P('seq', 'tp'), may hold values from -6 to 6
- cache_len: int32 [64], replicated, may hold values from 0 to 16, as said below
- out_weight: bfloat16 [1024, 2048], P('tp'), may hold values from -0.1875 to 0.1875
- norm_gain: bfloat16 [2048], replicated, may hold values from 0.099609375 to 1.8984375
- router: bfloat16 [2048, 64], replicated, may hold values from -2 to 2
- expert_ids: int32 [8192, 6], P('seq'), may hold values from 0 to 63, all different within a row; in each aligned block of 128 rows (0 to 127, 128 to 255, ...) at most 18 rows name the same one
- w_gate: bfloat16 [64, 2048, 1408], P('seq', None, 'tp'), may hold values from -0.125 to 0.125
- w_up: bfloat16 [64, 2048, 1408], P('seq', None, 'tp'), may hold values from -0.125 to 0.125
- w_down: bfloat16 [64, 1408, 2048], P('seq', None, 'tp'), may hold values from -0.15625 to 0.15625
- w_shared_gate: bfloat16 [2048, 1408], P('seq', 'tp'), may hold values from -0.125 to 0.125
- w_shared_up: bfloat16 [2048, 1408], P('seq', 'tp'), may hold values from -0.125 to 0.125
- w_shared_down: bfloat16 [1408, 2048], P('tp', 'seq'), may hold values from -0.15625 to 0.15625
Outputs:
- mixed: bfloat16 [8192, 2048], P('seq', 'tp')
Inputs may be any that keep to these rules, and one draw needn't show every extreme that they name: `cache_len`: some cache block has all 16 rows valid and another has none. `expert_ids`: each row names 6 different experts; the rows of one device name no expert more than 18 times, a bound that some block reaches.
All inputs are finite; a program needn't handle non-finite values.
Results may differ from a plain program's by a relative error of at most 0.013.
Values may be sent and summed in bfloat16 or wider, within the bound.
No kernel may reach another device: no remote copies, remote signals or barrier semaphores. Data moves between devices by JAX's collectives and lax.ppermute only.
A program may use at most 64 MiB of HBM per device.

v0:
```python
import math
import jax
import jax.numpy as jnp
from jax import lax
from jax.sharding import PartitionSpec as P

D = 2048
HD = 128
TOPK = 6


def expert_rows(rows, gate_w, up_w, down_w):
    sources, items = (rows.shape[0], rows.shape[1])
    flat_rows = rows.reshape(sources * items, rows.shape[2])
    gate_pre = jnp.dot(flat_rows, gate_w[0], preferred_element_type=jnp.float32)
    up_pre = jnp.dot(flat_rows, up_w[0], preferred_element_type=jnp.float32)
    inner_units = (
        (jax.nn.silu(gate_pre) * up_pre)
        .astype(jnp.bfloat16)
        .reshape(sources, items, gate_pre.shape[1])
    )
    inner_all = lax.all_gather(inner_units, "tp", axis=2, tiled=True)
    output = jnp.dot(
        inner_all.reshape(sources * items, inner_all.shape[2]),
        down_w[0],
        preferred_element_type=jnp.float32,
    )
    output = output.astype(jnp.bfloat16).reshape(sources, items, down_w.shape[2])
    return lax.all_to_all(output, "seq", split_axis=0, concat_axis=0, tiled=True)


def local(
    resid,
    query,
    key_new,
    value_new,
    key_cache,
    value_cache,
    cache_len,
    out_weight,
    norm_gain,
    router,
    expert_ids,
    w_gate,
    w_up,
    w_down,
    w_shared_gate,
    w_shared_up,
    w_shared_down,
):
    tok_rows = query.shape[0]
    heads_here = query.shape[1] // HD
    block_rows = key_cache.shape[0]
    seq_index = lax.axis_index("seq")
    tp_index = lax.axis_index("tp")
    width = D // lax.axis_size("tp")
    cache_keys, cache_values, fresh_keys, fresh_values = (
        lax.all_gather(key_cache, "seq", axis=0, tiled=True),
        lax.all_gather(value_cache, "seq", axis=0, tiled=True),
        lax.all_gather(key_new, "seq", axis=0, tiled=True),
        lax.all_gather(value_new, "seq", axis=0, tiled=True),
    )
    all_keys = jnp.concatenate([cache_keys, fresh_keys], 0)
    all_values = jnp.concatenate([cache_values, fresh_values], 0)
    span = all_keys.shape[0]
    scores = jnp.einsum(
        "qhd,khd->hqk",
        query.reshape(tok_rows, heads_here, HD),
        all_keys.reshape(span, heads_here, HD),
        preferred_element_type=jnp.float32,
    ) / math.sqrt(HD)
    cache_span = cache_keys.shape[0]
    cache_open = (jnp.arange(block_rows, dtype=jnp.int32)[None, :] < cache_len[:, None]).reshape(
        cache_span
    )
    query_place = seq_index * tok_rows + jnp.arange(tok_rows)
    fresh_open = jnp.arange(fresh_keys.shape[0])[None, :] <= query_place[:, None]
    visible = jnp.concatenate(
        [jnp.broadcast_to(cache_open[None, :], (tok_rows, cache_span)), fresh_open], 1
    )
    scores = jnp.where(visible[None], scores, -jnp.inf)
    top_score = jnp.max(scores, axis=-1, keepdims=True)
    weights = jnp.exp(scores - top_score)
    probs = (weights / jnp.sum(weights, axis=-1, keepdims=True)).astype(jnp.bfloat16)
    attn = jnp.einsum(
        "hqk,khd->qhd",
        probs,
        all_values.reshape(span, heads_here, HD),
        preferred_element_type=jnp.float32,
    )
    attn = attn.astype(jnp.bfloat16).reshape(tok_rows, heads_here * HD)
    partial_out = jnp.dot(attn, out_weight, preferred_element_type=jnp.float32)
    hidden_state = resid.astype(jnp.float32) + lax.psum(partial_out, "tp")
    mean_square = jnp.mean(hidden_state * hidden_state, axis=-1, keepdims=True)
    normed = (hidden_state * lax.rsqrt(mean_square + 1e-06) * norm_gain.astype(jnp.float32)).astype(
        jnp.bfloat16
    )
    own_hidden = lax.dynamic_slice_in_dim(hidden_state, tp_index * width, width, 1)
    logits = jnp.dot(normed, router, preferred_element_type=jnp.float32)
    expert_count = router.shape[1]
    expert_range = jnp.arange(expert_count, dtype=jnp.int32)
    picked = jnp.sum(
        jnp.where(expert_ids[:, :, None] == expert_range[None, None, :], logits[:, None, :], 0.0),
        axis=-1,
    )
    gates = jax.nn.softmax(picked, axis=-1)
    shared_gate = jnp.dot(
        normed,
        lax.all_gather(w_shared_gate, "seq", axis=0, tiled=True),
        preferred_element_type=jnp.float32,
    )
    shared_up = jnp.dot(
        normed,
        lax.all_gather(w_shared_up, "seq", axis=0, tiled=True),
        preferred_element_type=jnp.float32,
    )
    shared_inner = (jax.nn.silu(shared_gate) * shared_up).astype(jnp.bfloat16)
    shared_terms = jnp.dot(
        shared_inner,
        lax.all_gather(w_shared_down, "seq", axis=1, tiled=True),
        preferred_element_type=jnp.float32,
    )
    shared_own = lax.psum_scatter(
        shared_terms.astype(jnp.bfloat16), "tp", scatter_dimension=1, tiled=True
    ).astype(jnp.float32)
    capacity = max(2, 3 * tok_rows * TOPK // (2 * expert_count))
    flat_ids = expert_ids.reshape(tok_rows * TOPK)
    one_hot = (flat_ids[:, None] == expert_range[None, :]).astype(jnp.int32)
    before = jnp.cumsum(one_hot, axis=0) - one_hot
    slot = jnp.sum(one_hot * before, axis=1)
    dest = flat_ids * capacity + slot
    source_row = jnp.repeat(jnp.arange(tok_rows, dtype=jnp.int32), TOPK)
    buffer = jnp.zeros((expert_count * capacity, D), jnp.bfloat16).at[dest].set(normed[source_row])
    buffer = buffer.reshape(expert_count, capacity, D)
    returned = expert_rows(
        lax.all_to_all(buffer, "seq", split_axis=0, concat_axis=0, tiled=True), w_gate, w_up, w_down
    )
    picked_rows = returned.reshape(expert_count * capacity, width)[dest]
    weighted = picked_rows.astype(jnp.float32) * gates.reshape(tok_rows * TOPK)[:, None]
    routed = jnp.sum(weighted.reshape(tok_rows, TOPK, width), axis=1)
    return (own_hidden + shared_own + routed).astype(jnp.bfloat16)


def solution(mesh):
    return jax.shard_map(
        local,
        mesh=mesh,
        in_specs=(
            P("seq", None),
            P("seq", "tp"),
            P("seq", "tp"),
            P("seq", "tp"),
            P("seq", "tp"),
            P("seq", "tp"),
            P(),
            P("tp", None),
            P(),
            P(),
            P("seq", None),
            P("seq", None, "tp"),
            P("seq", None, "tp"),
            P("seq", None, "tp"),
            P("seq", "tp"),
            P("seq", "tp"),
            P("tp", "seq"),
        ),
        out_specs=P("seq", "tp"),
        check_vma=False,
    )
```

profile of v0, /device:TPU:16, one launch (start us, length us, event | category | flops | bytes accessed | tf_op | source)
XLA Modules:
  0.0 870.4 jit_solution(12710250860430260462)
XLA Ops:
  8.9 76.9 %all_gather.26 = bf16[1024,128]{1,0:T(8,128)(2,1)S(1)} all-gather(bf16[16,128]{1,0:T(8,128)(2,1)} %param.21), channel_id=1, replica_groups=mesh['seq'=64,'tp'=8] {'seq'}, dimensions={0}, use_global_device_ids=true | all-gather | bytes 266240 | tf_op jit(solution)/shard_map/all_gather | solution.py:58
  85.9 75.4 %all_gather.24 = bf16[1024,128]{1,0:T(8,128)(2,1)S(1)} all-gather(bf16[16,128]{1,0:T(8,128)(2,1)} %param.22), channel_id=1, replica_groups=mesh['seq'=64,'tp'=8] {'seq'}, dimensions={0}, use_global_device_ids=true | all-gather | bytes 266240 | tf_op jit(solution)/shard_map/all_gather | solution.py:59
  162.0 9.6 %fusion.46 = (f32[128]{0:T(128)S(1)}, f32[128,9216]{0,1:T(8,128)S(1)}) fusion(bf16[128,128]{1,0:T(8,128)(2,1)} %param.18, bf16[8192,128]{1,0:T(8,128)(2,1)} %all-gather.6.cloned.1.call-done, bf16[1024,128]{1,0:T(8,128)(2,1)S(1)} %all_gather.26, pred[128,8192]{0,1:T(32,128)(4,1)S(1)} %iota_compare_fusion, pred[9216]{0:T(1024)(128)(4,1)S(1)} %pad.2.clone), kind=kOutput, calls=%fused_computation.71 | convolution fusion | flops 311426944 | bytes 8168960 | tf_op jit(solution)/shard_map/qhd,khd->hqk/dot_general | solution.py:66
  171.6 2.1 copy-done.1
  175.0 8.1 all-gather.4.cloned.1.call-done
  183.2 5.3 fusion.22
  191.9 89.2 %all-reduce.2.cloned.1.call-done = f32[128,2048]{1,0:T(8,128)} async-done(((f32[128,2048]{1,0:T(8,128)}), f32[128,2048]{1,0:T(8,128)}) %all-reduce.2.cloned.1.call-update) | async-done | bytes 1048592 | tf_op jit(solution)/shard_map/psum | solution.py:93
  282.8 23.4 %scatter_custom_fusion = bf16[1152,2048]{1,0:T(8,128)(2,1)} fusion(s32[768]{0:T(1024)S(1)} %fusion.40, bf16[128,2048]{1,0:T(8,128)(2,1)S(1)} %multiply_convert_fusion, s32[1024]{0:T(1024)S(1)} %pad_clamp_fusion.1, bf16[]{:T(256)} %constant.44.clone.1), kind=kCustom, calls=%fused_computation.10 | custom fusion | bytes 4718594 | tf_op jit(solution)/shard_map/scatter | solution.py:133
  306.2 7.6 reshape.188
  313.8 168.2 %all_to_all.10 = bf16[64,18,2048]{2,1,0:T(8,128)(2,1)} all-to-all(bf16[64,18,2048]{2,1,0:T(8,128)(2,1)} %reshape.188), channel_id=1, replica_groups=mesh['seq'=64,'tp'=8] {'seq'}, dimensions={0} | all-to-all | bytes 9437184 | tf_op jit(solution)/shard_map/all_to_all | solution.py:136
  482.0 7.8 reshape.189
  489.8 4.2 fusion.26
  498.2 2.8 copy.41
  501.1 85.8 %all_gather.28 = bf16[2048,176]{1,0:T(8,128)(2,1)S(1)} all-gather(bf16[32,176]{1,0:T(8,128)(2,1)S(1)} %copy-done.5), channel_id=1, replica_groups=mesh['seq'=64,'tp'=8] {'seq'}, dimensions={0}, use_global_device_ids=true | all-gather | bytes 732160 | tf_op jit(solution)/shard_map/all_gather | solution.py:109
  586.8 79.7 %all_gather.29 = bf16[2048,176]{1,0:T(8,128)(2,1)S(1)} all-gather(bf16[32,176]{1,0:T(8,128)(2,1)S(1)} %copy-done.6), channel_id=1, replica_groups=mesh['seq'=64,'tp'=8] {'seq'}, dimensions={0}, use_global_device_ids=true | all-gather | bytes 732160 | tf_op jit(solution)/shard_map/all_gather | solution.py:114
  666.6 89.7 %all_gather.30 = bf16[176,2048]{0,1:T(8,128)(2,1)} all-gather(bf16[176,32]{0,1:T(8,128)(2,1)S(1)} %copy-done.7), channel_id=1, replica_groups=mesh['seq'=64,'tp'=8] {'seq'}, dimensions={1}, use_global_device_ids=true | all-gather | bytes 732160 | tf_op jit(solution)/shard_map/all_gather | solution.py:120
  756.8 13.3 %copy.42 = bf16[64,18,1408]{2,1,0:T(8,128)(2,1)} copy(bf16[64,18,1408]{0,1,2:T(8,128)(2,1)} %all-gather.8.cloned.1.call-done) | data formatting | bytes 6488064 | tf_op jit(solution)/shard_map/all_gather | solution.py:22
  770.2 5.8 reshape.191
  775.9 3.8 convolution_convert_fusion
  781.8 22.7 %all-to-all-start.1 = ((bf16[64,18,256]{2,1,0:T(8,128)(2,1)}), bf16[64,18,256]{2,1,0:T(8,128)(2,1)}, u32[]{:S(2)}, u32[]{:S(2)}) async-start(bf16[64,18,256]{2,1,0:T(8,128)(2,1)} %reshape.192), calls=%async_computation.2 | async-start | bytes 1572864 | tf_op jit(solution)/shard_map/all_to_all | solution.py:29
  804.6 3.2 convolution_convert_fusion.1
  809.3 19.2 %all-to-all-done.1 = bf16[64,18,256]{2,1,0:T(8,128)(2,1)} async-done(((bf16[64,18,256]{2,1,0:T(8,128)(2,1)}), bf16[64,18,256]{2,1,0:T(8,128)(2,1)}, u32[]{:S(2)}, u32[]{:S(2)}) %all-to-all-start.1) | async-done | bytes 589856 | tf_op jit(solution)/shard_map/all_to_all | solution.py:29
  829.8 3.3 gather_fusion
  834.6 27.8 %reduce-scatter.2.cloned.1.call-done = bf16[128,256]{1,0:T(8,128)(2,1)} async-done(((bf16[128,2048]{1,0:T(8,128)(2,1)}), bf16[128,256]{1,0:T(8,128)(2,1)}) %reduce-scatter.2.cloned.1.call-update) | async-done | bytes 65552 | tf_op jit(solution)/shard_map/reduce_scatter | solution.py:123
  (77 shorter events, 21.8 us)
Async XLA Ops:
  6.5 769.4 %copy-start = (bf16[1,1408,256]{2,1,0:T(8,128)(2,1)S(1)}, bf16[1,1408,256]{2,1,0:T(8,128)(2,1)}, u32[]{:S(2)}) copy-start(bf16[1,1408,256]{2,1,0:T(8,128)(2,1)} %param.30) | copy-start | bytes 2162692
  6.5 155.5 %all-gather.6.cloned.1.call-start = ((), (), s32[]{:S(2)}) async-start(), calls=%async_computation.4 | async-start | bytes 2129920 | tf_op jit(solution)/shard_map/all_gather | solution.py:60
  7.3 175.9 %all-gather.4.cloned.1.call-start = ((), (), s32[]{:S(2)}) async-start(), calls=%async_computation.3 | async-start | bytes 2129920 | tf_op jit(solution)/shard_map/all_gather | solution.py:61
  8.0 273.1 %all-reduce.2.cloned.1.call-start = ((), (), s32[]{:S(2)}) async-start(), calls=%async_computation.5 | async-start | bytes 2097152 | tf_op jit(solution)/shard_map/psum | solution.py:93
  171.6 2.1 copy-start.1
  171.6 11.5 %copy-start.11 = (bf16[128,2048]{1,0:T(8,128)(2,1)S(1)}, bf16[128,2048]{1,0:T(8,128)(2,1)}, u32[]{:S(2)}) copy-start(bf16[128,2048]{1,0:T(8,128)(2,1)} %param.24) | copy-start | bytes 1572868
  175.0 13.5 %copy-start.4 = (s32[128,6]{0,1:T(8,128)S(1)}, s32[128,6]{0,1:T(8,128)}, u32[]{:S(2)}) copy-start(s32[128,6]{0,1:T(8,128)} %param.27) | copy-start | bytes 9220
  175.0 13.9 %copy-start.8 = (bf16[2048]{0:T(1024)(128)(2,1)S(1)}, bf16[2048]{0:T(1024)(128)(2,1)}, u32[]{:S(2)}) copy-start(bf16[2048]{0:T(1024)(128)(2,1)} %param.25) | copy-start | bytes 12292
  175.0 106.1 %copy-start.3 = (bf16[128,2048]{1,0:T(8,128)(2,1)S(1)}, bf16[128,2048]{1,0:T(8,128)(2,1)}, u32[]{:S(2)}) copy-start(bf16[128,2048]{1,0:T(8,128)(2,1)} %param.17) | copy-start | bytes 1572868
  188.5 568.3 %all-gather.8.cloned.1.call-start = ((), (), s32[]{:S(2)}) async-start(), calls=%async_computation.7 | async-start | bytes 9732096 | tf_op jit(solution)/shard_map/all_gather | solution.py:22
  482.0 7.8 copy-start.9
  489.8 4.2 copy-start.2
  489.8 4.2 copy-start.10
  495.7 5.4 copy-start.5
  495.7 91.1 %copy-start.6 = (bf16[32,176]{1,0:T(8,128)(2,1)S(1)}, bf16[32,176]{1,0:T(8,128)(2,1)}, u32[]{:S(2)}) copy-start(bf16[32,176]{1,0:T(8,128)(2,1)} %param.32) | copy-start | bytes 33796
  495.7 170.8 %copy-start.7 = (bf16[176,32]{0,1:T(8,128)(2,1)S(1)}, bf16[176,32]{0,1:T(8,128)(2,1)}, u32[]{:S(2)}) copy-start(bf16[176,32]{0,1:T(8,128)(2,1)} %param.33) | copy-start | bytes 33796
  781.8 46.7 %all-to-all-start.1 = ((bf16[64,18,256]{2,1,0:T(8,128)(2,1)}), bf16[64,18,256]{2,1,0:T(8,128)(2,1)}, u32[]{:S(2)}, u32[]{:S(2)}) async-start(bf16[64,18,256]{2,1,0:T(8,128)(2,1)} %reshape.192), calls=%async_computation.2 | async-start | bytes 1572864 | tf_op jit(solution)/shard_map/all_to_all | solution.py:29
  804.5 57.9 %reduce-scatter.2.cloned.1.call-start = ((), (), s32[]{:S(2)}) async-start(), calls=%async_computation.6 | async-start | bytes 589824 | tf_op jit(solution)/shard_map/reduce_scatter | solution.py:123
Sparse Core Ops, SparseCore 0:
  10.7 88.5 all-gather.5
  102.6 80.4 all-gather.3
  188.6 92.4 all-reduce.1
  501.2 226.0 all-gather.7
  807.9 54.4 reduce-scatter.1
where the time goes:
time: 872 us; the launch traced here: 870 us
  blocking collectives  576 us (66%)
  waiting for transfers between devices  146 us (17%)
  local copies, waits for them, and re-layouts  74.3 us (9%)
  matrix products  29.6 us (3%)
  starting transfers between devices  22.9 us (3%)
  between operations  13.5 us (2%)
    all_to_all x1, blocking collectives, local(): lax.all_to_all(buffer, 'seq', split_axis=0, concat_axis=0, tiled=True)  168 us
    all_gather x1, blocking collectives, local(): lax.all_gather(w_shared_down, 'seq', axis=1, tiled=True)  89.7 us
    psum x1, waiting for transfers between devices, local(): hidden_state = resid.astype(jnp.float32) + lax.psum(partial_out, 'tp')  89.2 us
    all_gather x1, blocking collectives, local(): lax.all_gather(w_shared_gate, 'seq', axis=0, tiled=True)  85.8 us
    all_gather x1, blocking collectives, local(): lax.all_gather(w_shared_up, 'seq', axis=0, tiled=True)  79.7 us
    all_gather x1, blocking collectives, local(): lax.all_gather(key_cache, 'seq', axis=0, tiled=True)  76.9 us
    all_gather x1, blocking collectives, local(): lax.all_gather(value_cache, 'seq', axis=0, tiled=True)  75.4 us
    reduce_scatter x1, waiting for transfers between devices, local(): lax.psum_scatter(shared_terms.astype(jnp.bfloat16), 'tp', scatter_dimensi...  27.8 us
  transfers between devices with their start and end apart: 6, of which 4 were waited for; matrix products, arithmetic and copies ran while one was open for 3% of the time, Pallas kernels for 0%

commit v1 on v0

--- a/solution.py
+++ b/solution.py
@@ -90,7 +90,8 @@
     )
     attn = attn.astype(jnp.bfloat16).reshape(tok_rows, heads_here * HD)
     partial_out = jnp.dot(attn, out_weight, preferred_element_type=jnp.float32)
-    hidden_state = resid.astype(jnp.float32) + lax.psum(partial_out, "tp")
+    start_frames_on = lambda x_local: lax.all_gather(x_local, "tp").sum(axis=0)
+    hidden_state = resid.astype(jnp.float32) + start_frames_on(partial_out)
     mean_square = jnp.mean(hidden_state * hidden_state, axis=-1, keepdims=True)
     normed = (hidden_state * lax.rsqrt(mean_square + 1e-06) * norm_gain.astype(jnp.float32)).astype(
         jnp.bfloat16

time: 872 us -> 946 us (1.085)
  the two profiles are of different devices: /device:TPU:16 before, /device:TPU:240 now
where the time goes in v1:
time: 946 us; the launch traced here: 945 us
  blocking collectives  573 us (61%)
  waiting for transfers between devices  224 us (24%)
  local copies, waits for them, and re-layouts  74 us (8%)
  matrix products  29.7 us (3%)
  starting transfers between devices  19.5 us (2%)
  between operations  13.5 us (1%)
  other arithmetic  11.3 us (1%)
    all_gather x1, waiting for transfers between devices, local(): start_frames_on = lambda x_local: lax.all_gather(x_local, 'tp').sum(axis=0)  174 us
    all_to_all x1, blocking collectives, local(): lax.all_to_all(buffer, 'seq', split_axis=0, concat_axis=0, tiled=True)  168 us
    all_gather x1, blocking collectives, local(): lax.all_gather(w_shared_down, 'seq', axis=1, tiled=True)  88.6 us
    all_gather x1, blocking collectives, local(): lax.all_gather(w_shared_up, 'seq', axis=0, tiled=True)  86.6 us
    all_gather x1, blocking collectives, local(): lax.all_gather(value_cache, 'seq', axis=0, tiled=True)  79.7 us
    all_gather x1, blocking collectives, local(): lax.all_gather(w_shared_gate, 'seq', axis=0, tiled=True)  77.7 us
    all_gather x1, blocking collectives, local(): lax.all_gather(key_cache, 'seq', axis=0, tiled=True)  72.6 us
    reduce_scatter x1, waiting for transfers between devices, local(): lax.psum_scatter(shared_terms.astype(jnp.bfloat16), 'tp', scatter_dimensi...  29.9 us
  transfers between devices with their start and end apart: 6, of which 4 were waited for; matrix products, arithmetic and copies ran while one was open for 3% of the time, Pallas kernels for 0%

profile of v1, /device:TPU:240, one launch (start us, length us, event | category | flops | bytes accessed | tf_op | source)
XLA Modules:
  0.0 945.1 jit_solution(1285677586280921838)
XLA Ops:
  8.9 72.6 %all_gather.32 = bf16[1024,128]{1,0:T(8,128)(2,1)S(1)} all-gather(bf16[16,128]{1,0:T(8,128)(2,1)} %param.21), channel_id=1, replica_groups=mesh['seq'=64,'tp'=8] {'seq'}, dimensions={0}, use_global_device_ids=true | all-gather | bytes 266240 | tf_op jit(solution)/shard_map/all_gather | solution.py:58
  81.5 79.7 %all_gather.30 = bf16[1024,128]{1,0:T(8,128)(2,1)S(1)} all-gather(bf16[16,128]{1,0:T(8,128)(2,1)} %param.22), channel_id=1, replica_groups=mesh['seq'=64,'tp'=8] {'seq'}, dimensions={0}, use_global_device_ids=true | all-gather | bytes 266240 | tf_op jit(solution)/shard_map/all_gather | solution.py:59
  161.9 9.6 %fusion.46 = (f32[128]{0:T(128)S(1)}, f32[128,9216]{0,1:T(8,128)S(1)}) fusion(bf16[128,128]{1,0:T(8,128)(2,1)} %param.18, bf16[8192,128]{1,0:T(8,128)(2,1)} %all-gather.8.cloned.1.call-done, bf16[1024,128]{1,0:T(8,128)(2,1)S(1)} %all_gather.32, pred[128,8192]{0,1:T(32,128)(4,1)S(1)} %iota_compare_fusion, pred[9216]{0:T(1024)(128)(4,1)S(1)} %pad.2.clone), kind=kOutput, calls=%fused_computation.71 | convolution fusion | flops 311426944 | bytes 8168960 | tf_op jit(solution)/shard_map/qhd,khd->hqk/dot_general | solution.py:66
  174.9 2.7 all-gather.6.cloned.1.call-done
  177.7 5.4 fusion.22
  186.3 174.3 %all-gather.12.cloned.1.call-done = f32[1024,2048]{1,0:T(8,128)} async-done(((f32[128,2048]{1,0:T(8,128)}), f32[1024,2048]{1,0:T(8,128)}) %all-gather.12.cloned.1.call-update) | async-done | bytes 8388624 | tf_op jit(solution)/shard_map/all_gather | solution.py:93
  360.6 4.2 reduce_sum.66
  365.2 23.4 %scatter_custom_fusion = bf16[1152,2048]{1,0:T(8,128)(2,1)} fusion(s32[768]{0:T(1024)S(1)} %fusion.40, bf16[128,2048]{1,0:T(8,128)(2,1)S(1)} %multiply_convert_fusion, s32[1024]{0:T(1024)S(1)} %pad_clamp_fusion.1, bf16[]{:T(256)} %constant.44.clone.1), kind=kCustom, calls=%fused_computation.10 | custom fusion | bytes 4718594 | tf_op jit(solution)/shard_map/scatter | solution.py:134
  388.6 7.6 reshape.188
  396.2 167.9 %all_to_all.10 = bf16[64,18,2048]{2,1,0:T(8,128)(2,1)} all-to-all(bf16[64,18,2048]{2,1,0:T(8,128)(2,1)} %reshape.188), channel_id=1, replica_groups=mesh['seq'=64,'tp'=8] {'seq'}, dimensions={0} | all-to-all | bytes 9437184 | tf_op jit(solution)/shard_map/all_to_all | solution.py:137
  564.1 7.8 reshape.189
  571.9 4.2 fusion.26
  580.4 2.8 copy.41
  583.2 77.7 %all_gather.36 = bf16[2048,176]{1,0:T(8,128)(2,1)S(1)} all-gather(bf16[32,176]{1,0:T(8,128)(2,1)S(1)} %copy-done.5), channel_id=1, replica_groups=mesh['seq'=64,'tp'=8] {'seq'}, dimensions={0}, use_global_device_ids=true | all-gather | bytes 732160 | tf_op jit(solution)/shard_map/all_gather | solution.py:110
  660.9 86.6 %all_gather.37 = bf16[2048,176]{1,0:T(8,128)(2,1)S(1)} all-gather(bf16[32,176]{1,0:T(8,128)(2,1)S(1)} %copy-done.6), channel_id=1, replica_groups=mesh['seq'=64,'tp'=8] {'seq'}, dimensions={0}, use_global_device_ids=true | all-gather | bytes 732160 | tf_op jit(solution)/shard_map/all_gather | solution.py:115
  747.5 88.6 %all_gather.38 = bf16[176,2048]{0,1:T(8,128)(2,1)} all-gather(bf16[176,32]{0,1:T(8,128)(2,1)S(1)} %copy-done.7), channel_id=1, replica_groups=mesh['seq'=64,'tp'=8] {'seq'}, dimensions={1}, use_global_device_ids=true | all-gather | bytes 732160 | tf_op jit(solution)/shard_map/all_gather | solution.py:121
  836.6 13.1 %copy.42 = bf16[64,18,1408]{2,1,0:T(8,128)(2,1)} copy(bf16[64,18,1408]{0,1,2:T(8,128)(2,1)} %all-gather.10.cloned.1.call-done) | data formatting | bytes 6488064 | tf_op jit(solution)/shard_map/all_gather | solution.py:22
  849.7 5.8 reshape.191
  855.5 3.8 convolution_convert_fusion
  861.3 19.1 %all-to-all-start.1 = ((bf16[64,18,256]{2,1,0:T(8,128)(2,1)}), bf16[64,18,256]{2,1,0:T(8,128)(2,1)}, u32[]{:S(2)}, u32[]{:S(2)}) async-start(bf16[64,18,256]{2,1,0:T(8,128)(2,1)} %reshape.192), calls=%async_computation.2 | async-start | bytes 1572864 | tf_op jit(solution)/shard_map/all_to_all | solution.py:29
  880.7 3.2 convolution_convert_fusion.1
  885.4 15.7 %all-to-all-done.1 = bf16[64,18,256]{2,1,0:T(8,128)(2,1)} async-done(((bf16[64,18,256]{2,1,0:T(8,128)(2,1)}), bf16[64,18,256]{2,1,0:T(8,128)(2,1)}, u32[]{:S(2)}, u32[]{:S(2)}) %all-to-all-start.1) | async-done | bytes 589856 | tf_op jit(solution)/shard_map/all_to_all | solution.py:29
  902.4 3.3 gather_fusion
  907.2 29.9 %reduce-scatter.2.cloned.1.call-done = bf16[128,256]{1,0:T(8,128)(2,1)} async-done(((bf16[128,2048]{1,0:T(8,128)(2,1)}), bf16[128,256]{1,0:T(8,128)(2,1)}) %reduce-scatter.2.cloned.1.call-update) | async-done | bytes 65552 | tf_op jit(solution)/shard_map/reduce_scatter | solution.py:124
  (78 shorter events, 22.8 us)
Async XLA Ops:
  6.5 848.9 %copy-start = (bf16[1,1408,256]{2,1,0:T(8,128)(2,1)S(1)}, bf16[1,1408,256]{2,1,0:T(8,128)(2,1)}, u32[]{:S(2)}) copy-start(bf16[1,1408,256]{2,1,0:T(8,128)(2,1)} %param.30) | copy-start | bytes 2162692
  6.5 155.4 %all-gather.8.cloned.1.call-start = ((), (), s32[]{:S(2)}) async-start(), calls=%async_computation.4 | async-start | bytes 2129920 | tf_op jit(solution)/shard_map/all_gather | solution.py:60
  7.3 170.4 %all-gather.6.cloned.1.call-start = ((), (), s32[]{:S(2)}) async-start(), calls=%async_computation.3 | async-start | bytes 2129920 | tf_op jit(solution)/shard_map/all_gather | solution.py:61
  8.0 352.6 %all-gather.12.cloned.1.call-start = ((), (), s32[]{:S(2)}) async-start(), calls=%async_computation.7 | async-start | bytes 9437184 | tf_op jit(solution)/shard_map/all_gather | solution.py:93
  171.5 2.1 copy-start.1
  171.5 6.1 copy-start.11
  174.9 8.2 copy-start.4
  174.9 8.6 copy-start.8
  183.1 653.5 %all-gather.10.cloned.1.call-start = ((), (), s32[]{:S(2)}) async-start(), calls=%async_computation.6 | async-start | bytes 9732096 | tf_op jit(solution)/shard_map/all_gather | solution.py:22
  360.6 4.2 copy-start.3
  564.1 7.8 copy-start.9
  571.9 4.2 copy-start.2
  571.9 4.2 copy-start.10
  577.9 5.4 copy-start.5
  577.9 83.0 %copy-start.6 = (bf16[32,176]{1,0:T(8,128)(2,1)S(1)}, bf16[32,176]{1,0:T(8,128)(2,1)}, u32[]{:S(2)}) copy-start(bf16[32,176]{1,0:T(8,128)(2,1)} %param.32) | copy-start | bytes 33796
  577.9 169.6 %copy-start.7 = (bf16[176,32]{0,1:T(8,128)(2,1)S(1)}, bf16[176,32]{0,1:T(8,128)(2,1)}, u32[]{:S(2)}) copy-start(bf16[176,32]{0,1:T(8,128)(2,1)} %param.33) | copy-start | bytes 33796
  861.3 39.8 %all-to-all-start.1 = ((bf16[64,18,256]{2,1,0:T(8,128)(2,1)}), bf16[64,18,256]{2,1,0:T(8,128)(2,1)}, u32[]{:S(2)}, u32[]{:S(2)}) async-start(bf16[64,18,256]{2,1,0:T(8,128)(2,1)} %reshape.192), calls=%async_computation.2 | async-start | bytes 1572864 | tf_op jit(solution)/shard_map/all_to_all | solution.py:29
  880.4 56.7 %reduce-scatter.2.cloned.1.call-start = ((), (), s32[]{:S(2)}) async-start(), calls=%async_computation.5 | async-start | bytes 589824 | tf_op jit(solution)/shard_map/reduce_scatter | solution.py:124
Sparse Core Ops, SparseCore 0:
  10.7 83.0 all-gather.7
  97.2 80.4 all-gather.5
  183.2 177.3 all-gather.11
  583.4 190.9 all-gather.9
  884.1 52.9 reduce-scatter.1
